TPU v7x, 128 devices: a whole 4x4x4 slice. The times are simulated.
128 devices in a mesh: rows: 16 (over y, x), cols: 8 (over z, core).
Axes of the slice: x: 4, y: 4, z: 4, core: 2. Of those that a mesh axis runs over, the one named last changes fastest.
Arguments:
- ensemble: bfloat16 [64, 768, 1024], P(None, 'rows', 'cols'), may hold values from -6 to 6
- row_profile: bfloat16 [768, 16384], P('rows'), may hold values from 0.0072021484 to 0.071777344
- col_profile: bfloat16 [1024, 16384], P('cols'), may hold values from 0.006225586 to 0.0625
- obs_owned: float32 [128, 384], P(('rows', 'cols')), may hold values from -18 to 18
- noise_owned: float32 [128, 384], P(('rows', 'cols')), may hold values from 40.96 to 409.6
- block_owner: int32 [128], replicated, may hold values from 0 to 127, as said below
Outputs:
- updated: bfloat16 [64, 768, 1024], P(None, 'rows', 'cols')
Inputs may be any that keep to these rules, and one draw needn't show every extreme that they name: `block_owner`: each of the 128 devices owns at most 3 detector blocks, and some devices own exactly 3, some own 1 and some own none.
All inputs are finite; a program needn't handle non-finite values.
Results may differ from a plain program's by a relative error of at most 0.0011.
Values sent between devices are 32-bit elements; how exact they have to be, the bound alone decides.
A program may use at most 128 MiB of HBM per device.

v0:
```python
import math
import jax
import jax.numpy as jnp
from jax import lax
from jax.sharding import PartitionSpec as P

MEMBERS = 64
BLOCK = 128
CAP = 3


def partial_blocks(flat_field, row_prof, col_prof, first_block, block_count):
    group_size = math.gcd(block_count, 8)
    group_count = block_count // group_size
    span_cols = group_size * BLOCK
    local_rows = row_prof.shape[0]

    def group_terms(step_at):
        first_col = (first_block + step_at * group_size) * BLOCK
        col_part = lax.dynamic_slice_in_dim(col_prof, first_col, span_cols, 1)
        row_part = lax.dynamic_slice_in_dim(row_prof, first_col, span_cols, 1).astype(jnp.float32)
        along_cols = jnp.dot(flat_field, col_part, preferred_element_type=jnp.float32)
        along_cols = along_cols.reshape(MEMBERS, local_rows, span_cols)
        summed = jnp.sum(along_cols * row_part[None], axis=1)
        return summed.reshape(MEMBERS, group_size, BLOCK).transpose(1, 0, 2)

    terms = lax.map(group_terms, jnp.arange(group_count, dtype=jnp.int32))
    return terms.reshape(block_count, MEMBERS, BLOCK)


def member_stats(predictions, observed, weights):
    member_mean = jnp.mean(predictions, axis=1, keepdims=True)
    anomalies = (predictions - member_mean) / math.sqrt(MEMBERS - 1)
    residuals = observed[:, None, :] - predictions
    scaled = anomalies * weights[:, None, :]
    spread_mat = jnp.einsum("sjd,skd->jk", scaled, anomalies, precision=lax.Precision.HIGHEST)
    innovation = jnp.einsum("sjd,skd->jk", scaled, residuals, precision=lax.Precision.HIGHEST)
    return (spread_mat, innovation)


def on_device(ensemble, row_profile, col_profile, obs_owned, noise_owned, block_owner):
    own_index = lax.axis_index(("rows", "cols"))
    devices = lax.axis_size(("rows", "cols"))
    blocks = col_profile.shape[1] // BLOCK
    local_rows = ensemble.shape[1]
    local_cols = ensemble.shape[2]
    flat_field = ensemble.reshape(MEMBERS * local_rows, local_cols)
    block_index = jnp.arange(blocks, dtype=jnp.int32)
    same_owner = block_owner[None, :] == block_owner[:, None]
    earlier = block_index[None, :] < block_index[:, None]
    slot_rank = jnp.sum((same_owner & earlier).astype(jnp.int32), axis=1)
    obs_slots = obs_owned.reshape(CAP, BLOCK)
    noise_slots = noise_owned.reshape(CAP, BLOCK)
    partials = partial_blocks(flat_field, row_profile, col_profile, 0, blocks)
    owner_grid = jnp.arange(devices, dtype=jnp.int32)[:, None, None]
    slot_grid = jnp.arange(CAP, dtype=jnp.int32)[None, :, None]
    slot_hit = (block_owner[None, None, :] == owner_grid) & (slot_rank[None, None, :] == slot_grid)
    slot_valid = jnp.any(slot_hit, axis=2)
    slot_block = jnp.sum(jnp.where(slot_hit, block_index[None, None, :], 0), axis=2)
    send_buffer = jnp.where(slot_valid[:, :, None, None], partials[slot_block], 0.0)
    predictions = jnp.sum(
        lax.all_to_all(send_buffer, ("rows", "cols"), split_axis=0, concat_axis=0, tiled=True),
        axis=0,
    )
    owned_count = jnp.sum((block_owner == own_index).astype(jnp.int32))
    live_slot = jnp.arange(CAP, dtype=jnp.int32) < owned_count
    weights = jnp.where(live_slot[:, None], 1.0 / noise_slots, 0.0)
    spread_mat, innovation = member_stats(predictions, obs_slots, weights)
    spread_mat, innovation = lax.psum((spread_mat, innovation), ("rows", "cols"))
    eye_mat = jnp.eye(MEMBERS, dtype=jnp.float32)
    factor = jnp.linalg.cholesky(eye_mat + spread_mat)
    gain_weights = jax.scipy.linalg.cho_solve((factor, True), innovation)
    field_flat = ensemble.astype(jnp.float32).reshape(MEMBERS, -1)
    member_mean = jnp.mean(field_flat, axis=0, keepdims=True)
    anomalies = (field_flat - member_mean) / math.sqrt(MEMBERS - 1)
    moved = field_flat + jnp.dot(gain_weights.T, anomalies, precision=lax.Precision.HIGHEST)
    return moved.reshape(ensemble.shape).astype(jnp.bfloat16)


def solution(mesh):
    in_specs = (
        P(None, "rows", "cols"),
        P("rows", None),
        P("cols", None),
        P(("rows", "cols"), None),
        P(("rows", "cols"), None),
        P(),
    )
    out_specs = P(None, "rows", "cols")
    return jax.shard_map(
        on_device, mesh=mesh, in_specs=in_specs, out_specs=out_specs, check_vma=False
    )
```

profile of v0, /device:TPU:1, one launch (start us, length us, event | category | flops | bytes accessed | tf_op | source)
XLA Modules:
  0.0 768.0 jit_solution(12466156515473649168)
XLA Ops:
  1.9 479.6 %while.12 = (s32[]{:T(128)}, f32[16,8,64,128]{3,2,1,0:T(8,128)}, s32[16]{0:T(128)S(1)}, bf16[128,16384]{1,0:T(8,128)(2,1)}, bf16[3072,128]{1,0:T(8,128)(2,1)}, /...) while((s32[]{:T(128)}, f32[16,8,64,128]{3,2,1,0:T(8,128)}, ...), condition=%wide.region_4.5_spmd, body=%wide.region_2.4_spmd.sunk | while | flops 811581440 | bytes 53182640 | solution.py:27
  3.3 7.6 convolution_bitcast_fusion.4
  10.9 12.6 %copy.39 = f32[3072,1024]{1,0:T(8,128)} copy(f32[3072,1024]{0,1:T(8,128)} %convolution_bitcast_fusion.4) | data formatting | bytes 25165824 | tf_op jit(solution)/shard_map/while/body/eval_jaxpr/dot_general | solution.py:22
  24.4 6.6 multiply_reduce_fusion.2
  33.3 7.6 convolution_bitcast_fusion.4
  40.9 12.6 %copy.39 = f32[3072,1024]{1,0:T(8,128)} copy(f32[3072,1024]{0,1:T(8,128)} %convolution_bitcast_fusion.4) | data formatting | bytes 25165824 | tf_op jit(solution)/shard_map/while/body/eval_jaxpr/dot_general | solution.py:22
  54.4 6.6 multiply_reduce_fusion.2
  63.2 7.6 convolution_bitcast_fusion.4
  70.8 12.6 %copy.39 = f32[3072,1024]{1,0:T(8,128)} copy(f32[3072,1024]{0,1:T(8,128)} %convolution_bitcast_fusion.4) | data formatting | bytes 25165824 | tf_op jit(solution)/shard_map/while/body/eval_jaxpr/dot_general | solution.py:22
  84.3 6.6 multiply_reduce_fusion.2
  93.2 7.6 convolution_bitcast_fusion.4
  100.8 12.6 %copy.39 = f32[3072,1024]{1,0:T(8,128)} copy(f32[3072,1024]{0,1:T(8,128)} %convolution_bitcast_fusion.4) | data formatting | bytes 25165824 | tf_op jit(solution)/shard_map/while/body/eval_jaxpr/dot_general | solution.py:22
  114.3 6.6 multiply_reduce_fusion.2
  123.2 7.6 convolution_bitcast_fusion.4
  130.8 12.6 %copy.39 = f32[3072,1024]{1,0:T(8,128)} copy(f32[3072,1024]{0,1:T(8,128)} %convolution_bitcast_fusion.4) | data formatting | bytes 25165824 | tf_op jit(solution)/shard_map/while/body/eval_jaxpr/dot_general | solution.py:22
  144.3 6.6 multiply_reduce_fusion.2
  153.2 7.6 convolution_bitcast_fusion.4
  160.8 12.6 %copy.39 = f32[3072,1024]{1,0:T(8,128)} copy(f32[3072,1024]{0,1:T(8,128)} %convolution_bitcast_fusion.4) | data formatting | bytes 25165824 | tf_op jit(solution)/shard_map/while/body/eval_jaxpr/dot_general | solution.py:22
  183.1 7.6 convolution_bitcast_fusion.4
  190.8 12.6 %copy.39 = f32[3072,1024]{1,0:T(8,128)} copy(f32[3072,1024]{0,1:T(8,128)} %convolution_bitcast_fusion.4) | data formatting | bytes 25165824 | tf_op jit(solution)/shard_map/while/body/eval_jaxpr/dot_general | solution.py:22
  204.3 6.6 multiply_reduce_fusion.2
  213.1 7.6 convolution_bitcast_fusion.4
  220.7 12.6 %copy.39 = f32[3072,1024]{1,0:T(8,128)} copy(f32[3072,1024]{0,1:T(8,128)} %convolution_bitcast_fusion.4) | data formatting | bytes 25165824 | tf_op jit(solution)/shard_map/while/body/eval_jaxpr/dot_general | solution.py:22
  234.2 6.6 multiply_reduce_fusion.2
  243.1 7.6 convolution_bitcast_fusion.4
  250.7 12.6 %copy.39 = f32[3072,1024]{1,0:T(8,128)} copy(f32[3072,1024]{0,1:T(8,128)} %convolution_bitcast_fusion.4) | data formatting | bytes 25165824 | tf_op jit(solution)/shard_map/while/body/eval_jaxpr/dot_general | solution.py:22
  264.2 6.6 multiply_reduce_fusion.2
  273.1 7.6 convolution_bitcast_fusion.4
  280.7 12.6 %copy.39 = f32[3072,1024]{1,0:T(8,128)} copy(f32[3072,1024]{0,1:T(8,128)} %convolution_bitcast_fusion.4) | data formatting | bytes 25165824 | tf_op jit(solution)/shard_map/while/body/eval_jaxpr/dot_general | solution.py:22
  303.0 7.6 convolution_bitcast_fusion.4
  310.7 12.6 %copy.39 = f32[3072,1024]{1,0:T(8,128)} copy(f32[3072,1024]{0,1:T(8,128)} %convolution_bitcast_fusion.4) | data formatting | bytes 25165824 | tf_op jit(solution)/shard_map/while/body/eval_jaxpr/dot_general | solution.py:22
  324.2 6.6 multiply_reduce_fusion.2
  333.0 7.6 convolution_bitcast_fusion.4
  340.6 12.6 %copy.39 = f32[3072,1024]{1,0:T(8,128)} copy(f32[3072,1024]{0,1:T(8,128)} %convolution_bitcast_fusion.4) | data formatting | bytes 25165824 | tf_op jit(solution)/shard_map/while/body/eval_jaxpr/dot_general | solution.py:22
  354.1 6.6 multiply_reduce_fusion.2
  363.0 7.6 convolution_bitcast_fusion.4
  370.6 12.6 %copy.39 = f32[3072,1024]{1,0:T(8,128)} copy(f32[3072,1024]{0,1:T(8,128)} %convolution_bitcast_fusion.4) | data formatting | bytes 25165824 | tf_op jit(solution)/shard_map/while/body/eval_jaxpr/dot_general | solution.py:22
  392.9 7.6 convolution_bitcast_fusion.4
  400.6 12.6 %copy.39 = f32[3072,1024]{1,0:T(8,128)} copy(f32[3072,1024]{0,1:T(8,128)} %convolution_bitcast_fusion.4) | data formatting | bytes 25165824 | tf_op jit(solution)/shard_map/while/body/eval_jaxpr/dot_general | solution.py:22
  422.9 7.6 convolution_bitcast_fusion.4
  430.5 12.6 %copy.39 = f32[3072,1024]{1,0:T(8,128)} copy(f32[3072,1024]{0,1:T(8,128)} %convolution_bitcast_fusion.4) | data formatting | bytes 25165824 | tf_op jit(solution)/shard_map/while/body/eval_jaxpr/dot_general | solution.py:22
  452.9 7.6 convolution_bitcast_fusion.4
  460.5 12.6 %copy.39 = f32[3072,1024]{1,0:T(8,128)} copy(f32[3072,1024]{0,1:T(8,128)} %convolution_bitcast_fusion.4) | data formatting | bytes 25165824 | tf_op jit(solution)/shard_map/while/body/eval_jaxpr/dot_general | solution.py:22
  482.0 8.1 %gather_fusion = f32[384,64,128]{2,1,0:T(8,128)} fusion(f32[128,64,128]{2,1,0:T(8,128)} %bitcast.75, s32[1024]{0:T(1024)S(1)} %pad_clamp_fusion), kind=kCustom, calls=%fused_computation | custom fusion | bytes 25167360 | tf_op jit(solution)/shard_map/gather | solution.py:60
  490.1 10.2 %broadcast_select_fusion = f32[128,3,64,128]{3,2,1,0:T(8,128)} fusion(f32[128,3,64,128]{3,2,1,0:T(8,128)} %bitcast.71, pred[128,3]{1,0:T(8,128)(4,1)S(1)} %copy.15), kind=kLoop, calls=%fused_computation.9 | loop fusion | flops 3145728 | bytes 25166208 | tf_op jit(solution)/shard_map/jit(_where)/select_n | solution.py:60
  500.3 11.9 %all-to-all-start = ((f32[128,3,64,128]{3,2,1,0:T(8,128)}), f32[128,3,64,128]{3,2,1,0:T(8,128)}, u32[]{:S(2)}, u32[]{:S(2)}) async-start(f32[128,3,64,128]{3,2,1,0:T(8,128)} %broadcast_select_fusion), calls=%async_computation | async-start | bytes 25165824 | tf_op jit(solution)/shard_map/all_to_all | solution.py:62
  514.0 160.1 %all-to-all-done = f32[128,3,64,128]{3,2,1,0:T(8,128)} async-done(((f32[128,3,64,128]{3,2,1,0:T(8,128)}), f32[128,3,64,128]{3,2,1,0:T(8,128)}, u32[]{:S(2)}, u32[]{:S(2)}) %all-to-all-start) | async-done | bytes 12582944 | tf_op jit(solution)/shard_map/all_to_all | solution.py:62
  681.0 70.9 %all-reduce = (f32[64,64]{1,0:T(8,128)S(1)}, f32[64,64]{1,0:T(8,128)S(1)}) all-reduce(f32[64,64]{1,0:T(8,128)S(1)} %convolution_bitcast_fusion.1, f32[64,64]{1,0:T(8,128)S(1)} %convolution_bitcast_fusion.2), channel_id=1, replica_groups=mesh['rows'=16,'cols'=8] {'rows','cols'}, use_global_device_ids=true, to_apply=%region_12.13 | all-reduce | flops 8192 | bytes 65536 | tf_op jit(solution)/shard_map/psum | solution.py:69
  (114 shorter events, 104.9 us)
Async XLA Ops:
  500.3 11.9 %copy-start = (bf16[3072,128]{1,0:T(8,128)(2,1)S(1)}, bf16[3072,128]{1,0:T(8,128)(2,1)}, u32[]{:S(2)}) copy-start(bf16[3072,128]{1,0:T(8,128)(2,1)} %get-tuple-element.174) | copy-start | bytes 2359300
  500.3 12.1 %copy-start.2 = (f32[1,384]{1,0:T(1,128)S(1)}, f32[1,384]{1,0:T(1,128)}, u32[]{:S(2)}) copy-start(f32[1,384]{1,0:T(1,128)} %param.11) | copy-start | bytes 4612
  500.3 12.1 %copy-start.3 = (s32[128]{0:T(128)S(1)}, s32[128]{0:T(128)}, u32[]{:S(2)}) copy-start(s32[128]{0:T(128)} %param.13) | copy-start | bytes 1540
  500.3 13.4 %copy-start.1 = (f32[1,384]{1,0:T(1,128)S(1)}, f32[1,384]{1,0:T(1,128)}, u32[]{:S(2)}) copy-start(f32[1,384]{1,0:T(1,128)} %param.12) | copy-start | bytes 4612
  500.3 173.8 %all-to-all-start = ((f32[128,3,64,128]{3,2,1,0:T(8,128)}), f32[128,3,64,128]{3,2,1,0:T(8,128)}, u32[]{:S(2)}, u32[]{:S(2)}) async-start(f32[128,3,64,128]{3,2,1,0:T(8,128)} %broadcast_select_fusion), calls=%async_computation | async-start | bytes 25165824 | tf_op jit(solution)/shard_map/all_to_all | solution.py:62
where the time goes:
time: 772 us; the launch traced here: 768 us
  local copies, waits for them, and re-layouts  235 us (30%)
  waiting for transfers between devices  160 us (21%)
  other arithmetic  153 us (20%)
  matrix products  125 us (16%)
  blocking collectives  70.9 us (9%)
  starting transfers between devices  11.9 us (2%)
  loops' own time  11.5 us (1%)
    dot_general x16, local copies, waits for them, and re-layouts, group_terms(): jnp.dot(flat_field, col_part, preferred_element_type=jnp.float32)  201 us
    all_to_all x1, waiting for transfers between devices, on_device(): lax.all_to_all(send_buffer, ('rows', 'cols'), split_axis=0, concat_axis=0...  160 us
    dot_general x16, matrix products, group_terms(): jnp.dot(flat_field, col_part, preferred_element_type=jnp.float32)  122 us
    reduce_sum x16, other arithmetic, group_terms(): summed = jnp.sum(along_cols * row_part[None], axis=1)  106 us
    psum x1, blocking collectives, on_device(): lax.psum((spread_mat, innovation), ('rows', 'cols'))  70.9 us
  transfers between devices with their start and end apart: 1, of which 1 were waited for; matrix products, arithmetic and copies ran while one was open for 0% of the time, Pallas kernels for 0%

commit v1 on v0

--- a/solution.py
+++ b/solution.py
@@ -66,7 +66,7 @@
     live_slot = jnp.arange(CAP, dtype=jnp.int32) < owned_count
     weights = jnp.where(live_slot[:, None], 1.0 / noise_slots, 0.0)
     spread_mat, innovation = member_stats(predictions, obs_slots, weights)
-    spread_mat, innovation = lax.psum((spread_mat, innovation), ("rows", "cols"))
+    spread_mat, innovation = lax.psum(lax.psum((spread_mat, innovation), "rows"), "cols")
     eye_mat = jnp.eye(MEMBERS, dtype=jnp.float32)
     factor = jnp.linalg.cholesky(eye_mat + spread_mat)
     gain_weights = jax.scipy.linalg.cho_solve((factor, True), innovation)

time: 772 us -> 802 us (1.039)
  blocking collectives: 70.9 us -> 99.2 us
    psum x1 -> x2, blocking collectives: 70.9 us -> 99.2 us  [the longest x1 58.5 us: on_device(): lax.psum((spread_mat, innovation), 'rows')]
where the time goes in v1:
time: 802 us; the launch traced here: 796 us
  local copies, waits for them, and re-layouts  235 us (29%)
  waiting for transfers between devices  160 us (20%)
  other arithmetic  153 us (19%)
  matrix products  125 us (16%)
  blocking collectives  99.2 us (12%)
  starting transfers between devices  11.9 us (1%)
  loops' own time  11.5 us (1%)
    dot_general x16, local copies, waits for them, and re-layouts, group_terms(): jnp.dot(flat_field, col_part, preferred_element_type=jnp.float32)  201 us
    all_to_all x1, waiting for transfers between devices, on_device(): lax.all_to_all(send_buffer, ('rows', 'cols'), split_axis=0, concat_axis=0...  160 us
    dot_general x16, matrix products, group_terms(): jnp.dot(flat_field, col_part, preferred_element_type=jnp.float32)  122 us
    reduce_sum x16, other arithmetic, group_terms(): summed = jnp.sum(along_cols * row_part[None], axis=1)  106 us
    psum x1, blocking collectives, on_device(): lax.psum((spread_mat, innovation), 'rows')  58.5 us
    psum x1, blocking collectives, on_device(): lax.psum(lax.psum((spread_mat, innovation), 'rows'), 'cols')  40.8 us
  transfers between devices with their start and end apart: 1, of which 1 were waited for; matrix products, arithmetic and copies ran while one was open for 0% of the time, Pallas kernels for 0%

profile of v1, /device:TPU:1, one launch (start us, length us, event | category | flops | bytes accessed | tf_op | source)
XLA Modules:
  0.0 796.3 jit_solution(9917908438308344663)
XLA Ops:
  1.9 479.6 %while.12 = (s32[]{:T(128)}, f32[16,8,64,128]{3,2,1,0:T(8,128)}, s32[16]{0:T(128)S(1)}, bf16[128,16384]{1,0:T(8,128)(2,1)}, bf16[3072,128]{1,0:T(8,128)(2,1)}, /...) while((s32[]{:T(128)}, f32[16,8,64,128]{3,2,1,0:T(8,128)}, ...), condition=%wide.region_4.5_spmd, body=%wide.region_2.4_spmd.sunk | while | flops 811581440 | bytes 53182640 | solution.py:27
  3.3 7.6 convolution_bitcast_fusion.4
  10.9 12.6 %copy.39 = f32[3072,1024]{1,0:T(8,128)} copy(f32[3072,1024]{0,1:T(8,128)} %convolution_bitcast_fusion.4) | data formatting | bytes 25165824 | tf_op jit(solution)/shard_map/while/body/eval_jaxpr/dot_general | solution.py:22
  24.4 6.6 multiply_reduce_fusion.2
  33.3 7.6 convolution_bitcast_fusion.4
  40.9 12.6 %copy.39 = f32[3072,1024]{1,0:T(8,128)} copy(f32[3072,1024]{0,1:T(8,128)} %convolution_bitcast_fusion.4) | data formatting | bytes 25165824 | tf_op jit(solution)/shard_map/while/body/eval_jaxpr/dot_general | solution.py:22
  54.4 6.6 multiply_reduce_fusion.2
  63.2 7.6 convolution_bitcast_fusion.4
  70.8 12.6 %copy.39 = f32[3072,1024]{1,0:T(8,128)} copy(f32[3072,1024]{0,1:T(8,128)} %convolution_bitcast_fusion.4) | data formatting | bytes 25165824 | tf_op jit(solution)/shard_map/while/body/eval_jaxpr/dot_general | solution.py:22
  84.3 6.6 multiply_reduce_fusion.2
  93.2 7.6 convolution_bitcast_fusion.4
  100.8 12.6 %copy.39 = f32[3072,1024]{1,0:T(8,128)} copy(f32[3072,1024]{0,1:T(8,128)} %convolution_bitcast_fusion.4) | data formatting | bytes 25165824 | tf_op jit(solution)/shard_map/while/body/eval_jaxpr/dot_general | solution.py:22
  114.3 6.6 multiply_reduce_fusion.2
  123.2 7.6 convolution_bitcast_fusion.4
  130.8 12.6 %copy.39 = f32[3072,1024]{1,0:T(8,128)} copy(f32[3072,1024]{0,1:T(8,128)} %convolution_bitcast_fusion.4) | data formatting | bytes 25165824 | tf_op jit(solution)/shard_map/while/body/eval_jaxpr/dot_general | solution.py:22
  144.3 6.6 multiply_reduce_fusion.2
  153.2 7.6 convolution_bitcast_fusion.4
  160.8 12.6 %copy.39 = f32[3072,1024]{1,0:T(8,128)} copy(f32[3072,1024]{0,1:T(8,128)} %convolution_bitcast_fusion.4) | data formatting | bytes 25165824 | tf_op jit(solution)/shard_map/while/body/eval_jaxpr/dot_general | solution.py:22
  183.1 7.6 convolution_bitcast_fusion.4
  190.8 12.6 %copy.39 = f32[3072,1024]{1,0:T(8,128)} copy(f32[3072,1024]{0,1:T(8,128)} %convolution_bitcast_fusion.4) | data formatting | bytes 25165824 | tf_op jit(solution)/shard_map/while/body/eval_jaxpr/dot_general | solution.py:22
  204.3 6.6 multiply_reduce_fusion.2
  213.1 7.6 convolution_bitcast_fusion.4
  220.7 12.6 %copy.39 = f32[3072,1024]{1,0:T(8,128)} copy(f32[3072,1024]{0,1:T(8,128)} %convolution_bitcast_fusion.4) | data formatting | bytes 25165824 | tf_op jit(solution)/shard_map/while/body/eval_jaxpr/dot_general | solution.py:22
  234.2 6.6 multiply_reduce_fusion.2
  243.1 7.6 convolution_bitcast_fusion.4
  250.7 12.6 %copy.39 = f32[3072,1024]{1,0:T(8,128)} copy(f32[3072,1024]{0,1:T(8,128)} %convolution_bitcast_fusion.4) | data formatting | bytes 25165824 | tf_op jit(solution)/shard_map/while/body/eval_jaxpr/dot_general | solution.py:22
  264.2 6.6 multiply_reduce_fusion.2
  273.1 7.6 convolution_bitcast_fusion.4
  280.7 12.6 %copy.39 = f32[3072,1024]{1,0:T(8,128)} copy(f32[3072,1024]{0,1:T(8,128)} %convolution_bitcast_fusion.4) | data formatting | bytes 25165824 | tf_op jit(solution)/shard_map/while/body/eval_jaxpr/dot_general | solution.py:22
  303.0 7.6 convolution_bitcast_fusion.4
  310.7 12.6 %copy.39 = f32[3072,1024]{1,0:T(8,128)} copy(f32[3072,1024]{0,1:T(8,128)} %convolution_bitcast_fusion.4) | data formatting | bytes 25165824 | tf_op jit(solution)/shard_map/while/body/eval_jaxpr/dot_general | solution.py:22
  324.2 6.6 multiply_reduce_fusion.2
  333.0 7.6 convolution_bitcast_fusion.4
  340.6 12.6 %copy.39 = f32[3072,1024]{1,0:T(8,128)} copy(f32[3072,1024]{0,1:T(8,128)} %convolution_bitcast_fusion.4) | data formatting | bytes 25165824 | tf_op jit(solution)/shard_map/while/body/eval_jaxpr/dot_general | solution.py:22
  363.0 7.6 convolution_bitcast_fusion.4
  370.6 12.6 %copy.39 = f32[3072,1024]{1,0:T(8,128)} copy(f32[3072,1024]{0,1:T(8,128)} %convolution_bitcast_fusion.4) | data formatting | bytes 25165824 | tf_op jit(solution)/shard_map/while/body/eval_jaxpr/dot_general | solution.py:22
  392.9 7.6 convolution_bitcast_fusion.4
  400.6 12.6 %copy.39 = f32[3072,1024]{1,0:T(8,128)} copy(f32[3072,1024]{0,1:T(8,128)} %convolution_bitcast_fusion.4) | data formatting | bytes 25165824 | tf_op jit(solution)/shard_map/while/body/eval_jaxpr/dot_general | solution.py:22
  422.9 7.6 convolution_bitcast_fusion.4
  430.5 12.6 %copy.39 = f32[3072,1024]{1,0:T(8,128)} copy(f32[3072,1024]{0,1:T(8,128)} %convolution_bitcast_fusion.4) | data formatting | bytes 25165824 | tf_op jit(solution)/shard_map/while/body/eval_jaxpr/dot_general | solution.py:22
  452.9 7.6 convolution_bitcast_fusion.4
  460.5 12.6 %copy.39 = f32[3072,1024]{1,0:T(8,128)} copy(f32[3072,1024]{0,1:T(8,128)} %convolution_bitcast_fusion.4) | data formatting | bytes 25165824 | tf_op jit(solution)/shard_map/while/body/eval_jaxpr/dot_general | solution.py:22
  482.0 8.1 %gather_fusion = f32[384,64,128]{2,1,0:T(8,128)} fusion(f32[128,64,128]{2,1,0:T(8,128)} %bitcast.75, s32[1024]{0:T(1024)S(1)} %pad_clamp_fusion), kind=kCustom, calls=%fused_computation | custom fusion | bytes 25167360 | tf_op jit(solution)/shard_map/gather | solution.py:60
  490.1 10.2 %broadcast_select_fusion = f32[128,3,64,128]{3,2,1,0:T(8,128)} fusion(f32[128,3,64,128]{3,2,1,0:T(8,128)} %bitcast.71, pred[128,3]{1,0:T(8,128)(4,1)S(1)} %copy.15), kind=kLoop, calls=%fused_computation.9 | loop fusion | flops 3145728 | bytes 25166208 | tf_op jit(solution)/shard_map/jit(_where)/select_n | solution.py:60
  500.3 11.9 %all-to-all-start = ((f32[128,3,64,128]{3,2,1,0:T(8,128)}), f32[128,3,64,128]{3,2,1,0:T(8,128)}, u32[]{:S(2)}, u32[]{:S(2)}) async-start(f32[128,3,64,128]{3,2,1,0:T(8,128)} %broadcast_select_fusion), calls=%async_computation | async-start | bytes 25165824 | tf_op jit(solution)/shard_map/all_to_all | solution.py:62
  514.0 160.1 %all-to-all-done = f32[128,3,64,128]{3,2,1,0:T(8,128)} async-done(((f32[128,3,64,128]{3,2,1,0:T(8,128)}), f32[128,3,64,128]{3,2,1,0:T(8,128)}, u32[]{:S(2)}, u32[]{:S(2)}) %all-to-all-start) | async-done | bytes 12582944 | tf_op jit(solution)/shard_map/all_to_all | solution.py:62
  681.0 58.5 %all-reduce = (f32[64,64]{1,0:T(8,128)S(1)}, f32[64,64]{1,0:T(8,128)S(1)}) all-reduce(f32[64,64]{1,0:T(8,128)S(1)} %convolution_bitcast_fusion.1, f32[64,64]{1,0:T(8,128)S(1)} %convolution_bitcast_fusion.2), channel_id=1, replica_groups=mesh['rows'=16,'cols'=8] {'rows'}, use_global_device_ids=true, to_apply=%region_13.14 | all-reduce | flops 8192 | bytes 65536 | tf_op jit(solution)/shard_map/psum | solution.py:69
  739.4 40.8 %all-reduce.1 = (f32[64,64]{1,0:T(8,128)S(1)}, f32[64,64]{1,0:T(8,128)S(1)}) all-reduce(f32[64,64]{1,0:T(8,128)S(1)} %get-tuple-element.103, f32[64,64]{1,0:T(8,128)S(1)} %get-tuple-element.104), channel_id=1, replica_groups=mesh['rows'=16,'cols'=8] {'cols'}, use_global_device_ids=true, to_apply=%region_14.15 | all-reduce | flops 8192 | bytes 65536 | tf_op jit(solution)/shard_map/psum | solution.py:69
  (115 shorter events, 111.5 us)
Async XLA Ops:
  500.3 11.9 %copy-start = (bf16[3072,128]{1,0:T(8,128)(2,1)S(1)}, bf16[3072,128]{1,0:T(8,128)(2,1)}, u32[]{:S(2)}) copy-start(bf16[3072,128]{1,0:T(8,128)(2,1)} %get-tuple-element.176) | copy-start | bytes 2359300
  500.3 12.1 %copy-start.2 = (f32[1,384]{1,0:T(1,128)S(1)}, f32[1,384]{1,0:T(1,128)}, u32[]{:S(2)}) copy-start(f32[1,384]{1,0:T(1,128)} %param.11) | copy-start | bytes 4612
  500.3 12.1 %copy-start.3 = (s32[128]{0:T(128)S(1)}, s32[128]{0:T(128)}, u32[]{:S(2)}) copy-start(s32[128]{0:T(128)} %param.13) | copy-start | bytes 1540
  500.3 13.4 %copy-start.1 = (f32[1,384]{1,0:T(1,128)S(1)}, f32[1,384]{1,0:T(1,128)}, u32[]{:S(2)}) copy-start(f32[1,384]{1,0:T(1,128)} %param.12) | copy-start | bytes 4612
  500.3 173.8 %all-to-all-start = ((f32[128,3,64,128]{3,2,1,0:T(8,128)}), f32[128,3,64,128]{3,2,1,0:T(8,128)}, u32[]{:S(2)}, u32[]{:S(2)}) async-start(f32[128,3,64,128]{3,2,1,0:T(8,128)} %broadcast_select_fusion), calls=%async_computation | async-start | bytes 25165824 | tf_op jit(solution)/shard_map/all_to_all | solution.py:62
